TPU v7x, 128 devices: a whole 4x4x4 slice. The times are simulated.
128 devices in a mesh: expert: 4 (over z), panel: 32 (over y, x, core).
Axes of the slice: x: 4, y: 4, z: 4, core: 2. Of those that a mesh axis runs over, the one named last changes fastest.
Arguments:
- tokens: bfloat16 [4096, 6144], P(('expert', 'panel')), may hold values from -6 to 6
- routes: int32 [4096, 2], P(('expert', 'panel')), may hold values from 0 to 7, all different within a row; in each aligned block of 32 rows (0 to 31, 32 to 63, ...) at most 12 rows name the same one
- router_weights: float32 [4096, 2], P(('expert', 'panel')), may hold values from 0.05 to 0.95
Outputs:
- hessian: float32 [8, 6144, 6144], P('expert', 'panel')
Inputs may be any that keep to these rules, and one draw needn't show every extreme that they name: `routes`: each row names two different experts; among the 32 rows of one device no expert is named more than 12 times, a bound that some block reaches.
All inputs are finite; a program needn't handle non-finite values.
Results may differ from a plain program's by a relative error of at most 0.0036.
Values may be sent and summed in bfloat16 or wider, within the bound.
A program may use at most 192 MiB of HBM per device.

v0:
```python
import jax
import jax.numpy as jnp
from jax import lax
from jax.sharding import PartitionSpec as P

EXPERTS = 8
CAP = 12


def per_device(tokens, routes, router_weights):
    count, width = tokens.shape
    groups = lax.axis_size("expert")
    panels = lax.axis_size("panel")
    quarter = width // groups
    panel_width = width // panels
    scaling = float(groups * panels * CAP) ** (-0.5)
    rounded = router_weights.astype(jnp.bfloat16)
    ids = jnp.arange(64, dtype=jnp.int32)[None, :]
    zero = jnp.zeros((), jnp.bfloat16)
    dense = jnp.where(routes[:, 0:1] == ids, rounded[:, 0:1], zero) + jnp.where(
        routes[:, 1:2] == ids, rounded[:, 1:2], zero
    )
    seed = lax.all_to_all(
        tokens.reshape(count, groups, quarter), "expert", split_axis=1, concat_axis=0, tiled=True
    ).reshape(groups * count, quarter)
    columns = lax.all_gather(seed, "panel", axis=0, tiled=True)
    rows = jnp.concatenate(
        [
            tokens.reshape(count, panels, panel_width),
            jnp.broadcast_to(dense[:, None, :], (count, panels, 64)),
        ],
        axis=2,
    )
    rows = lax.all_to_all(rows, "panel", split_axis=1, concat_axis=0, tiled=True)
    rows = rows.reshape(panels * count, panel_width + 64)
    rows = lax.all_gather(rows, "expert", axis=0, tiled=True)
    rows = rows.reshape(groups, panels, count, panel_width + 64).transpose(3, 1, 0, 2)
    rows = rows.reshape(panel_width + 64, -1)
    weights = rows[panel_width : panel_width + EXPERTS]
    scaled = (weights[:, None, :] * rows[None, :panel_width, :]).reshape(-1, rows.shape[1])
    blocks = jnp.dot(scaled, columns, preferred_element_type=jnp.float32) * scaling
    blocks = blocks.astype(jnp.bfloat16).reshape(groups, EXPERTS // groups, panel_width, quarter)
    blocks = lax.all_to_all(blocks, "expert", split_axis=0, concat_axis=0, tiled=True)
    return blocks.transpose(1, 2, 0, 3).reshape(-1, panel_width, width).astype(jnp.float32)


def solution(mesh):
    placed = (
        P(("expert", "panel"), None),
        P(("expert", "panel"), None),
        P(("expert", "panel"), None),
    )
    return jax.shard_map(
        per_device,
        mesh=mesh,
        in_specs=placed,
        out_specs=P("expert", "panel", None),
        check_vma=False,
    )
```

profile of v0, /device:TPU:1, one launch (start us, length us, event | category | flops | bytes accessed | tf_op | source)
XLA Modules:
  0.0 222.1 jit_solution(15191602077753477741)
XLA Ops:
  6.5 0.0 all-gather.3.cloned.1.call-start
  6.5 0.7 convert_element_type.15
  7.2 0.8 slice_bitcast_fusion.3
  8.0 1.6 reshape.97
  9.6 0.1 fusion.3
  9.8 0.2 pad_maximum_fusion
  9.9 0.3 copy.15
  10.2 20.0 %all_to_all.35 = bf16[32,32,256]{2,0,1:T(8,128)(2,1)} all-to-all(bf16[32,32,256]{2,0,1:T(8,128)(2,1)S(1)} %copy.15), channel_id=1, replica_groups=mesh['expert'=4,'panel'=32] {'panel'}, dimensions={1} | all-to-all | bytes 1048576 | tf_op jit(solution)/shard_map/all_to_all | solution.py:34
  30.3 0.0 all-gather.3.cloned.1.call-update
  30.3 0.0 all-gather.5.cloned.1.call-start
  30.3 1.0 copy.27
  31.4 12.3 %all_to_all.36 = bf16[32,4,1536]{2,0,1:T(8,128)(2,1)} all-to-all(bf16[32,4,1536]{2,0,1:T(8,128)(2,1)S(1)} %bitcast.46), channel_id=1, replica_groups=mesh['expert'=4,'panel'=32] {'expert'}, dimensions={1} | all-to-all | bytes 786432 | tf_op jit(solution)/shard_map/all_to_all | solution.py:23
  43.7 0.0 all-gather.5.cloned.1.call-update
  43.7 18.0 %all-gather.3.cloned.1.call-done = bf16[4096,256]{1,0:T(8,128)(2,1)} async-done(((bf16[1024,256]{1,0:T(8,128)(2,1)}), bf16[4096,256]{1,0:T(8,128)(2,1)}) %all-gather.3.cloned.1.call-update) | async-done | bytes 2097168 | tf_op jit(solution)/shard_map/all_gather | solution.py:36
  61.7 1.8 copy.26
  63.6 0.4 slice.26
  64.0 0.3 copy.21
  64.3 2.7 %copy.18 = bf16[192,4096]{1,0:T(8,128)(2,1)} copy(bf16[192,4096]{0,1:T(8,128)(2,1)S(1)} %bitcast.38) | data formatting | bytes 3145728 | tf_op jit(solution)/shard_map/mul | solution.py:40
  67.0 6.8 %broadcast_multiply_fusion = bf16[8,192,4096]{2,1,0:T(8,128)(2,1)} fusion(bf16[192,4096]{1,0:T(8,128)(2,1)} %copy.18, bf16[8,4096]{1,0:T(8,128)(2,1)S(1)} %copy.21), kind=kLoop, calls=%fused_computation.3 | loop fusion | flops 6291456 | bytes 14221312 | tf_op jit(solution)/shard_map/mul | solution.py:40
  73.8 51.5 %all-gather.5.cloned.1.call-done = bf16[4096,1536]{1,0:T(8,128)(2,1)} async-done(((bf16[128,1536]{1,0:T(8,128)(2,1)}), bf16[4096,1536]{1,0:T(8,128)(2,1)}) %all-gather.5.cloned.1.call-update) | async-done | bytes 12582928 | tf_op jit(solution)/shard_map/all_gather | solution.py:26
  125.3 26.0 %fusion = bf16[1536,1536]{1,0:T(8,128)(2,1)S(1)} fusion(bf16[1536,4096]{1,0:T(8,128)(2,1)} %bitcast.39, bf16[4096,1536]{1,0:T(8,128)(2,1)} %all-gather.5.cloned.1.call-done), kind=kOutput, calls=%fused_computation.2 | convolution fusion | flops 19332071424 | bytes 29884416 | tf_op jit(solution)/shard_map/dot_general | solution.py:41
  151.4 57.9 %all_to_all.37 = bf16[4,2,192,1536]{3,2,1,0:T(8,128)(2,1)S(1)} all-to-all(bf16[4,2,192,1536]{3,2,1,0:T(8,128)(2,1)S(1)} %bitcast.40), channel_id=1, replica_groups=mesh['expert'=4,'panel'=32] {'expert'}, dimensions={0} | all-to-all | bytes 9437184 | tf_op jit(solution)/shard_map/all_to_all | solution.py:43
  209.3 1.3 convert_bitcast_fusion
  210.6 4.6 %copy.23 = f32[4,2,24,8,1536]{4,3,0,2,1:T(8,128)} copy(f32[4,2,24,8,1536]{4,3,2,1,0:T(8,128)S(1)} %convert_bitcast_fusion) | data formatting | bytes 18874368 | tf_op jit(solution)/shard_map/convert_element_type | solution.py:44
  (2 shorter events, 0.0 us)
Async XLA Ops:
  6.5 55.2 %all-gather.3.cloned.1.call-start = ((), (), s32[]{:S(2)}) async-start(), calls=%async_computation.3 | async-start | bytes 2621440 | tf_op jit(solution)/shard_map/all_gather | solution.py:36
  30.3 95.0 %all-gather.5.cloned.1.call-start = ((), (), s32[]{:S(2)}) async-start(), calls=%async_computation.4 | async-start | bytes 12976128 | tf_op jit(solution)/shard_map/all_gather | solution.py:26
Sparse Core Ops, SparseCore 0:
  30.4 31.2 all-gather.2
  64.0 61.3 all-gather.4
where the time goes:
time: 222 us
  blocking collectives  90.3 us (41%)
  waiting for transfers between devices  69.6 us (31%)
  matrix products  26 us (12%)
  local copies, waits for them, and re-layouts  13.6 us (6%)
  between operations  13.5 us (6%)
  other arithmetic  9.06 us (4%)
    all_to_all x1, blocking collectives, per_device(): lax.all_to_all(blocks, 'expert', split_axis=0, concat_axis=0, tiled=True)  57.9 us
    all_gather x1, waiting for transfers between devices, per_device(): columns = lax.all_gather(seed, 'panel', axis=0, tiled=True)  51.5 us
    dot_general x1, matrix products, per_device(): jnp.dot(scaled, columns, preferred_element_type=jnp.float32) * scaling  26 us
    all_to_all x1, blocking collectives, per_device(): lax.all_to_all(rows, 'panel', split_axis=1, concat_axis=0, tiled=True)  20 us
    all_gather x1, waiting for transfers between devices, per_device(): rows = lax.all_gather(rows, 'expert', axis=0, tiled=True)  18 us
    all_to_all x1, blocking collectives, per_device(): lax.all_to_all(tokens.reshape(count, groups, quarter), 'expert', split_ax...  12.3 us
    mul x1, other arithmetic, per_device(): weights[:, None, :] * rows[None, :panel_width, :]  6.83 us
    convert_element_type x1, local copies, waits for them, and re-layouts, per_device(): blocks.transpose(1, 2, 0, 3).reshape(-1, panel_width, width)  4.6 us
  transfers between devices with their start and end apart: 2, of which 2 were waited for; matrix products, arithmetic and copies ran while one was open for 6% of the time, Pallas kernels for 0%

commit v1 on v0

--- a/solution.py
+++ b/solution.py
@@ -33,7 +33,14 @@
     )
     rows = lax.all_to_all(rows, "panel", split_axis=1, concat_axis=0, tiled=True)
     rows = rows.reshape(panels * count, panel_width + 64)
-    rows = lax.all_gather(rows, "expert", axis=0, tiled=True)
+    devices = lax.axis_size("expert")
+    forward = [(i, (i + 1) % devices) for i in range(devices)]
+    pieces = [rows]
+    for hop in range(1, devices):
+        pieces = [lax.ppermute(pieces[0], "expert", forward), *pieces]
+    whole = jnp.concatenate(pieces, axis=0)
+    shift = (lax.axis_index("expert") + 1) * pieces[-1].shape[0]
+    rows = jnp.roll(whole, shift, axis=0)
     rows = rows.reshape(groups, panels, count, panel_width + 64).transpose(3, 1, 0, 2)
     rows = rows.reshape(panel_width + 64, -1)
     weights = rows[panel_width : panel_width + EXPERTS]

time: 222 us -> 198 us (0.89)
  the two profiles are of different devices: /device:TPU:1 before, /device:TPU:8 now
where the time goes in v1:
time: 198 us
  blocking collectives  89.9 us (45%)
  waiting for transfers between devices  45.3 us (23%)
  matrix products  26 us (13%)
  local copies, waits for them, and re-layouts  14.5 us (7%)
  between operations  13.5 us (7%)
  other arithmetic  7.57 us (4%)
    all_to_all x1, blocking collectives, per_device(): lax.all_to_all(blocks, 'expert', split_axis=0, concat_axis=0, tiled=True)  56.5 us
    ppermute x3, waiting for transfers between devices, per_device(): pieces = [lax.ppermute(pieces[0], 'expert', forward), *pieces]  45.3 us
    dot_general x1, matrix products, per_device(): jnp.dot(scaled, columns, preferred_element_type=jnp.float32) * scaling  26 us
    all_to_all x1, blocking collectives, per_device(): lax.all_to_all(rows, 'panel', split_axis=1, concat_axis=0, tiled=True)  20.1 us
    all_to_all x1, blocking collectives, per_device(): lax.all_to_all(tokens.reshape(count, groups, quarter), 'expert', split_ax...  13.3 us
    mul x1, other arithmetic, per_device(): weights[:, None, :] * rows[None, :panel_width, :]  5.34 us
    convert_element_type x1, local copies, waits for them, and re-layouts, per_device(): blocks.transpose(1, 2, 0, 3).reshape(-1, panel_width, width)  4.6 us
  transfers between devices with their start and end apart: 4, of which 3 were waited for; matrix products, arithmetic and copies ran while one was open for 8% of the time, Pallas kernels for 0%

profile of v1, /device:TPU:8, one launch (start us, length us, event | category | flops | bytes accessed | tf_op | source)
XLA Modules:
  0.0 197.8 jit_solution(9773385992295185005)
XLA Ops:
  6.5 0.0 all-gather.2.cloned.1.call-start
  6.5 1.0 copy.23
  7.6 13.3 %all_to_all.35 = bf16[32,4,1536]{2,0,1:T(8,128)(2,1)} all-to-all(bf16[32,4,1536]{2,0,1:T(8,128)(2,1)S(1)} %bitcast.45), channel_id=1, replica_groups=mesh['expert'=4,'panel'=32] {'expert'}, dimensions={1} | all-to-all | bytes 786432 | tf_op jit(solution)/shard_map/all_to_all | solution.py:23
  20.8 0.0 all-gather.2.cloned.1.call-update
  20.9 1.6 reshape.97
  22.5 0.7 convert_element_type.15
  23.2 0.8 slice_bitcast_fusion.3
  24.0 0.1 fusion.3
  24.1 0.2 pad_maximum_fusion
  24.3 0.3 copy.14
  24.6 20.1 %all_to_all.36 = bf16[32,32,256]{2,0,1:T(8,128)(2,1)S(1)} all-to-all(bf16[32,32,256]{2,0,1:T(8,128)(2,1)S(1)} %copy.14), channel_id=1, replica_groups=mesh['expert'=4,'panel'=32] {'panel'}, dimensions={1} | all-to-all | bytes 1048576 | tf_op jit(solution)/shard_map/all_to_all | solution.py:34
  44.6 0.8 collective-permute-start
  45.5 14.7 %collective-permute-done = bf16[1024,256]{1,0:T(8,128)(2,1)S(1)} collective-permute-done((bf16[1024,256]{1,0:T(8,128)(2,1)S(1)}, bf16[1024,256]{1,0:T(8,128)(2,1)S(1)}, u32[]{:S(2)}, u32[]{:S(2)}) %collective-permute-start) | collective-permute-done | bytes 524320 | tf_op jit(solution)/shard_map/ppermute | solution.py:40
  60.2 0.1 collective-permute-start.1
  60.3 15.6 %collective-permute-done.1 = bf16[1024,256]{1,0:T(8,128)(2,1)S(1)} collective-permute-done((bf16[1024,256]{1,0:T(8,128)(2,1)S(1)}, bf16[1024,256]{1,0:T(8,128)(2,1)S(1)}, u32[]{:S(2)}, u32[]{:S(2)}) %collective-permute-start.1) | collective-permute-done | bytes 524320 | tf_op jit(solution)/shard_map/ppermute | solution.py:40
  75.9 0.0 collective-permute-start.2
  75.9 15.0 %collective-permute-done.2 = bf16[1024,256]{1,0:T(8,128)(2,1)S(1)} collective-permute-done((bf16[1024,256]{1,0:T(8,128)(2,1)S(1)}, bf16[1024,256]{1,0:T(8,128)(2,1)S(1)}, u32[]{:S(2)}, u32[]{:S(2)}) %collective-permute-start.2) | collective-permute-done | bytes 524320 | tf_op jit(solution)/shard_map/ppermute | solution.py:40
  91.3 0.1 constant_dynamic-slice_fusion
  91.4 0.4 slice.26
  91.8 0.6 copy.15
  92.4 0.3 mul.31
  92.7 1.6 copy.16
  94.3 2.9 %copy.17 = bf16[192,4096]{1,0:T(8,128)(2,1)S(1)} copy(bf16[192,4096]{0,1:T(8,128)(2,1)} %bitcast.38) | data formatting | bytes 3145728 | tf_op jit(solution)/shard_map/mul | solution.py:47
  97.1 5.3 %broadcast_multiply_fusion = bf16[8,192,4096]{2,1,0:T(8,128)(2,1)} fusion(bf16[192,4096]{1,0:T(8,128)(2,1)S(1)} %copy.17, bf16[8,4096]{1,0:T(8,128)(2,1)S(1)} %mul.31), kind=kLoop, calls=%fused_computation.3 | loop fusion | flops 6291456 | bytes 14221312 | tf_op jit(solution)/shard_map/mul | solution.py:47
  102.5 0.0 all-gather.2.cloned.1.call-done
  102.5 26.0 %fusion = bf16[1536,1536]{1,0:T(8,128)(2,1)S(1)} fusion(bf16[1536,4096]{1,0:T(8,128)(2,1)} %bitcast.37, bf16[4096,1536]{1,0:T(8,128)(2,1)} %all-gather.2.cloned.1.call-done), kind=kOutput, calls=%fused_computation.2 | convolution fusion | flops 19332071424 | bytes 29884416 | tf_op jit(solution)/shard_map/dot_general | solution.py:48
  128.5 56.5 %all_to_all.37 = bf16[4,2,192,1536]{3,2,1,0:T(8,128)(2,1)S(1)} all-to-all(bf16[4,2,192,1536]{3,2,1,0:T(8,128)(2,1)S(1)} %bitcast.39), channel_id=1, replica_groups=mesh['expert'=4,'panel'=32] {'expert'}, dimensions={0} | all-to-all | bytes 9437184 | tf_op jit(solution)/shard_map/all_to_all | solution.py:50
  185.1 1.3 convert_bitcast_fusion
  186.4 4.6 %copy.21 = f32[4,2,24,8,1536]{4,3,0,2,1:T(8,128)} copy(f32[4,2,24,8,1536]{4,3,2,1,0:T(8,128)S(1)} %convert_bitcast_fusion) | data formatting | bytes 18874368 | tf_op jit(solution)/shard_map/convert_element_type | solution.py:51
  (10 shorter events, 0.3 us)
Async XLA Ops:
  6.5 95.9 %all-gather.2.cloned.1.call-start = ((), (), s32[]{:S(2)}) async-start(), calls=%async_computation.3 | async-start | bytes 12976128 | tf_op jit(solution)/shard_map/all_gather | solution.py:26
  44.6 15.5 %collective-permute-start = (bf16[1024,256]{1,0:T(8,128)(2,1)S(1)}, bf16[1024,256]{1,0:T(8,128)(2,1)S(1)}, u32[]{:S(2)}, u32[]{:S(2)}) collective-permute-start(bf16[1024,256]{1,0:T(8,128)(2,1)S(1)} %bitcast.40), channel_id=1, source_target_pairs={{0,32},{32,64},{64,96},{96,0},{1,33},{33,65},{65,97},{97,1},{2,34}... | collective-permute-start | bytes 1572872 | tf_op jit(solution)/shard_map/ppermute | solution.py:40
  60.2 15.7 %collective-permute-start.1 = (bf16[1024,256]{1,0:T(8,128)(2,1)S(1)}, bf16[1024,256]{1,0:T(8,128)(2,1)S(1)}, u32[]{:S(2)}, u32[]{:S(2)}) collective-permute-start(bf16[1024,256]{1,0:T(8,128)(2,1)S(1)} %collective-permute-done), channel_id=1, source_target_pairs={{0,32},{32,64},{64,96},{96,0},{1,33},{33,65},{65,97},{97,1},{2,34}... | collective-permute-start | bytes 1572872 | tf_op jit(solution)/shard_map/ppermute | solution.py:40
  75.9 15.0 %collective-permute-start.2 = (bf16[1024,256]{1,0:T(8,128)(2,1)S(1)}, bf16[1024,256]{1,0:T(8,128)(2,1)S(1)}, u32[]{:S(2)}, u32[]{:S(2)}) collective-permute-start(bf16[1024,256]{1,0:T(8,128)(2,1)S(1)} %collective-permute-done.1), channel_id=1, source_target_pairs={{0,32},{32,64},{64,96},{96,0},{1,33},{33,65},{65,97},{97,1},{2,34}... | collective-permute-start | bytes 1572872 | tf_op jit(solution)/shard_map/ppermute | solution.py:40
Sparse Core Ops, SparseCore 0:
  21.0 65.1 all-gather.1
